TPU v7x, 32 devices: a whole 2x2x4 slice. The times are simulated.
32 devices in a mesh: fsdp: 32 (over z, y, x, core).
Axes of the slice: x: 2, y: 2, z: 4, core: 2. Of those that a mesh axis runs over, the one named last changes fastest.
Arguments:
- tokens: bfloat16 [2, 32, 576, 1024], P(None, 'fsdp'), may hold values from -5 to 5
- lengths: int32 [2, 32], P(None, 'fsdp'), may hold values from 196 to 576, as said below
- cotangent: float32 [2, 32, 8, 1024], P(None, 'fsdp'), may hold values from -768 to 768
- ln1_gain: bfloat16 [1024], P('fsdp'), may hold values from 0.5 to 1.5
- ln1_bias: bfloat16 [1024], P('fsdp'), may hold values from -1.1953125 to 1.1953125
- w_qkv: bfloat16 [1024, 3072], P('fsdp'), may hold values from -0.25 to 0.25
- b_qv: bfloat16 [2048], P('fsdp'), may hold values from -1.1953125 to 1.1953125
- w_out: bfloat16 [1024, 1024], P('fsdp'), may hold values from -0.375 to 0.375
- b_out: bfloat16 [1024], P('fsdp'), may hold values from -1.1953125 to 1.1953125
- ln2_gain: bfloat16 [1024], P('fsdp'), may hold values from 0.5 to 1.5
- ln2_bias: bfloat16 [1024], P('fsdp'), may hold values from -1.1953125 to 1.1953125
- w_up: bfloat16 [1024, 4096], P('fsdp'), may hold values from -0.1875 to 0.1875
- b_up: bfloat16 [4096], P('fsdp'), may hold values from -1.1953125 to 1.1953125
- w_down: bfloat16 [4096, 1024], P('fsdp'), may hold values from -0.09375 to 0.09375
- b_down: bfloat16 [1024], P('fsdp'), may hold values from -1.1953125 to 1.1953125
- ln3_gain: bfloat16 [1024], P('fsdp'), may hold values from 0.5 to 1.5
- ln3_bias: bfloat16 [1024], P('fsdp'), may hold values from -1.1953125 to 1.1953125
- w_learn: bfloat16 [1024, 1024], P('fsdp'), may hold values from -0.1875 to 0.1875
- b_learn: bfloat16 [1024], P('fsdp'), may hold values from -1.1953125 to 1.1953125
- w_map: bfloat16 [1024, 8], P('fsdp'), may hold values from -0.75 to 0.75
Outputs:
- pooled: float32 [2, 32, 8, 1024], P(None, 'fsdp')
- d_tokens: float32 [2, 32, 576, 1024], P(None, 'fsdp')
- grad_ln1_gain: float32 [1024], P('fsdp')
- grad_ln1_bias: float32 [1024], P('fsdp')
- grad_w_qkv: float32 [1024, 3072], P('fsdp')
- grad_b_qv: float32 [2048], P('fsdp')
- grad_w_out: float32 [1024, 1024], P('fsdp')
- grad_b_out: float32 [1024], P('fsdp')
- grad_ln2_gain: float32 [1024], P('fsdp')
- grad_ln2_bias: float32 [1024], P('fsdp')
- grad_w_up: float32 [1024, 4096], P('fsdp')
- grad_b_up: float32 [4096], P('fsdp')
- grad_w_down: float32 [4096, 1024], P('fsdp')
- grad_b_down: float32 [1024], P('fsdp')
- grad_ln3_gain: float32 [1024], P('fsdp')
- grad_ln3_bias: float32 [1024], P('fsdp')
- grad_w_learn: float32 [1024, 1024], P('fsdp')
- grad_b_learn: float32 [1024], P('fsdp')
- grad_w_map: float32 [1024, 8], P('fsdp')
Inputs may be any that keep to these rules, and one draw needn't show every extreme that they name: `lengths`: each image has 196 or 576 patches; both counts occur in every draw.
All inputs are finite; a program needn't handle non-finite values.
Results may differ from a plain program's by a relative error of at most 0.013.
Values may be sent and summed in bfloat16 or wider, within the bound.
No kernel may reach another device: no remote copies, remote signals or barrier semaphores. Data moves between devices by JAX's collectives and lax.ppermute only.
A program may use at most 448 MiB of HBM per device.

v0:
```python
import jax
import jax.numpy as jnp
from jax import lax
from jax.sharding import PartitionSpec as P

D = 1024
HEADS = 16
HD = 64
EPSILON = 1e-06
SCALE = 0.125


def layer_norm(values, gain, shift):
    row_mean = jnp.mean(values, axis=-1, keepdims=True)
    centered = values - row_mean
    variance = jnp.mean(centered * centered, axis=-1, keepdims=True)
    return centered * lax.rsqrt(variance + EPSILON) * gain + shift


def norm_back(values, gain, shift, incoming):
    _, pull_back = jax.vjp(layer_norm, values, gain, shift)
    return pull_back(incoming)


def gelu_exact(values):
    return jax.nn.gelu(values, approximate=False)


def gelu_slope(values, incoming):
    _, pull_back = jax.vjp(gelu_exact, values)
    return pull_back(incoming)[0]


def product(left, right):
    return jnp.dot(left, right, preferred_element_type=jnp.float32)


def product_rows(left, right):
    return lax.dot_general(
        left, right, (((0,), (0,)), ((), ())), preferred_element_type=jnp.float32
    )


def product_back(left, right):
    return lax.dot_general(
        left, right, (((1,), (1,)), ((), ())), preferred_element_type=jnp.float32
    )


def attention_scores(queries, key_rows, slot_valid):
    scores = (
        jnp.einsum("qhd,khd->hqk", queries, key_rows, preferred_element_type=jnp.float32) * SCALE
    )
    return jnp.where(slot_valid[None, None, :], scores, -1e30)


def unflatten_all(flat_local, grads, devices):
    pieces = []
    offset = 0
    for item in grads:
        local_shape = (item.shape[0] // devices,) + item.shape[1:]
        count = item.size // devices
        pieces.append(flat_local[offset : offset + count].reshape(local_shape))
        offset = offset + count
    return tuple(pieces)


def image_forward(params, image_rows, length):
    (
        ln1_gain,
        ln1_bias,
        w_qkv,
        b_qv,
        w_out,
        b_out,
        ln2_gain,
        ln2_bias,
        w_up,
        b_up,
        w_down,
        b_down,
        ln3_gain,
        ln3_bias,
        w_learn,
        b_learn,
        w_map,
    ) = params
    slot_count = image_rows.shape[0]
    slot_valid = lax.iota(jnp.int32, slot_count) < length
    source = image_rows.astype(jnp.float32)
    hidden = layer_norm(source, ln1_gain.astype(jnp.float32), ln1_bias.astype(jnp.float32)).astype(
        jnp.bfloat16
    )
    qkv_rows = product(hidden, w_qkv)
    qv_bias = b_qv.astype(jnp.float32)
    queries = (qkv_rows[:, :D] + qv_bias[:D]).astype(jnp.bfloat16).reshape(slot_count, HEADS, HD)
    key_rows = qkv_rows[:, D : 2 * D].astype(jnp.bfloat16).reshape(slot_count, HEADS, HD)
    values = (
        (qkv_rows[:, 2 * D :] + qv_bias[D:]).astype(jnp.bfloat16).reshape(slot_count, HEADS, HD)
    )
    scores = attention_scores(queries, key_rows, slot_valid)
    row_top = jnp.max(scores, axis=-1, keepdims=True)
    row_total = jnp.sum(jnp.exp(scores - row_top), axis=-1, keepdims=True)
    log_total = row_top + jnp.log(row_total)
    probs_low = jnp.exp(scores - log_total).astype(jnp.bfloat16)
    attended = jnp.einsum("hqk,khd->qhd", probs_low, values, preferred_element_type=jnp.float32)
    attended = attended.reshape(slot_count, D).astype(jnp.bfloat16)
    middle = source + product(attended, w_out) + b_out.astype(jnp.float32)
    normed = layer_norm(middle, ln2_gain.astype(jnp.float32), ln2_bias.astype(jnp.float32)).astype(
        jnp.bfloat16
    )
    up_proj = product(normed, w_up) + b_up.astype(jnp.float32)
    up_act = gelu_exact(up_proj).astype(jnp.bfloat16)
    output = middle + product(up_act, w_down) + b_down.astype(jnp.float32)
    learn_in = layer_norm(
        output, ln3_gain.astype(jnp.float32), ln3_bias.astype(jnp.float32)
    ).astype(jnp.bfloat16)
    learn_mid = product(learn_in, w_learn) + b_learn.astype(jnp.float32)
    learn_act = gelu_exact(learn_mid).astype(jnp.bfloat16)
    logits = product(learn_act, w_map)
    pool_share = slot_valid.astype(jnp.float32) / length.astype(jnp.float32)
    pool_maps = jax.nn.sigmoid(logits) * pool_share[:, None]
    pooled = jnp.einsum("sm,sd->md", pool_maps, output, precision=lax.Precision.HIGHEST)
    saved = (
        queries,
        key_rows,
        values,
        log_total,
        attended,
        middle,
        normed,
        up_proj,
        up_act,
        output,
        learn_in,
        learn_mid,
        learn_act,
        logits,
    )
    return (pooled, saved)


def image_backward(params, image_rows, length, pool_grad, saved):
    (
        ln1_gain,
        ln1_bias,
        w_qkv,
        b_qv,
        w_out,
        b_out,
        ln2_gain,
        ln2_bias,
        w_up,
        b_up,
        w_down,
        b_down,
        ln3_gain,
        ln3_bias,
        w_learn,
        b_learn,
        w_map,
    ) = params
    (
        queries,
        key_rows,
        values,
        log_total,
        attended,
        middle,
        normed,
        up_proj,
        up_act,
        output,
        learn_in,
        learn_mid,
        learn_act,
        logits,
    ) = saved
    slot_count = image_rows.shape[0]
    slot_valid = lax.iota(jnp.int32, slot_count) < length
    source = image_rows.astype(jnp.float32)
    pool_share = slot_valid.astype(jnp.float32) / length.astype(jnp.float32)
    squashed = jax.nn.sigmoid(logits)
    pool_maps = squashed * pool_share[:, None]
    d_maps = jnp.einsum("sd,md->sm", output, pool_grad, precision=lax.Precision.HIGHEST)
    d_logits = (d_maps * pool_share[:, None] * squashed * (1.0 - squashed)).astype(jnp.bfloat16)
    d_output = jnp.einsum("sm,md->sd", pool_maps, pool_grad, precision=lax.Precision.HIGHEST)
    g_map = product_rows(learn_act, d_logits)
    d_learn = gelu_slope(learn_mid, product_back(d_logits, w_map)).astype(jnp.bfloat16)
    g_blearn = jnp.sum(d_learn.astype(jnp.float32), axis=0)
    g_wlearn = product_rows(learn_in, d_learn)
    d_norm3, g_ln3, h_ln3 = norm_back(
        output,
        ln3_gain.astype(jnp.float32),
        ln3_bias.astype(jnp.float32),
        product_back(d_learn, w_learn),
    )
    d_output = d_output + d_norm3
    d_mlp = d_output.astype(jnp.bfloat16)
    g_bdown = jnp.sum(d_mlp.astype(jnp.float32), axis=0)
    g_wdown = product_rows(up_act, d_mlp)
    d_up = gelu_slope(up_proj, product_back(d_mlp, w_down)).astype(jnp.bfloat16)
    g_bup = jnp.sum(d_up.astype(jnp.float32), axis=0)
    g_wup = product_rows(normed, d_up)
    d_norm2, g_ln2, h_ln2 = norm_back(
        middle, ln2_gain.astype(jnp.float32), ln2_bias.astype(jnp.float32), product_back(d_up, w_up)
    )
    d_middle = d_output + d_norm2
    d_branch = d_middle.astype(jnp.bfloat16)
    g_bout = jnp.sum(d_branch.astype(jnp.float32), axis=0)
    g_wout = product_rows(attended, d_branch)
    d_attn = product_back(d_branch, w_out).astype(jnp.bfloat16).reshape(slot_count, HEADS, HD)
    scores = attention_scores(queries, key_rows, slot_valid)
    probs = jnp.exp(scores - log_total)
    probs_low = probs.astype(jnp.bfloat16)
    d_values = jnp.einsum(
        "hqk,qhd->khd", probs_low, d_attn, preferred_element_type=jnp.float32
    ).astype(jnp.bfloat16)
    d_probs = jnp.einsum("qhd,khd->hqk", d_attn, values, preferred_element_type=jnp.float32)
    d_scores = (probs * (d_probs - jnp.sum(probs * d_probs, axis=-1, keepdims=True))).astype(
        jnp.bfloat16
    )
    d_queries = (
        jnp.einsum("hqk,khd->qhd", d_scores, key_rows, preferred_element_type=jnp.float32) * SCALE
    ).astype(jnp.bfloat16)
    d_keys = (
        jnp.einsum("hqk,qhd->khd", d_scores, queries, preferred_element_type=jnp.float32) * SCALE
    ).astype(jnp.bfloat16)
    d_qkv = jnp.concatenate(
        [
            d_queries.reshape(slot_count, D),
            d_keys.reshape(slot_count, D),
            d_values.reshape(slot_count, D),
        ],
        axis=1,
    )
    g_bqv = jnp.concatenate(
        [
            jnp.sum(d_queries.reshape(slot_count, D).astype(jnp.float32), axis=0),
            jnp.sum(d_values.reshape(slot_count, D).astype(jnp.float32), axis=0),
        ]
    )
    gain_one = ln1_gain.astype(jnp.float32)
    bias_one = ln1_bias.astype(jnp.float32)
    hidden = layer_norm(source, gain_one, bias_one).astype(jnp.bfloat16)
    g_wqkv = product_rows(hidden, d_qkv)
    d_norm1, g_ln1, h_ln1 = norm_back(source, gain_one, bias_one, product_back(d_qkv, w_qkv))
    d_image = d_middle + d_norm1
    grad_parts = (
        g_ln1,
        h_ln1,
        g_wqkv,
        g_bqv,
        g_wout,
        g_bout,
        g_ln2,
        h_ln2,
        g_wup,
        g_bup,
        g_wdown,
        g_bdown,
        g_ln3,
        h_ln3,
        g_wlearn,
        g_blearn,
        g_map,
    )
    return (d_image, grad_parts)


def body(
    tokens,
    lengths,
    cotangent,
    ln1_gain,
    ln1_bias,
    w_qkv,
    b_qv,
    w_out,
    b_out,
    ln2_gain,
    ln2_bias,
    w_up,
    b_up,
    w_down,
    b_down,
    ln3_gain,
    ln3_bias,
    w_learn,
    b_learn,
    w_map,
):
    shards = (
        ln1_gain,
        ln1_bias,
        w_qkv,
        b_qv,
        w_out,
        b_out,
        ln2_gain,
        ln2_bias,
        w_up,
        b_up,
        w_down,
        b_down,
        ln3_gain,
        ln3_bias,
        w_learn,
        b_learn,
        w_map,
    )
    devices = lax.axis_size("fsdp")
    micro_count = tokens.shape[0]
    pooled_parts = []
    grad_image_parts = []
    grad_total = None
    for micro_step in range(micro_count):
        forward_params = (
            lax.all_gather(shards[0], "fsdp", axis=0, tiled=True),
            lax.all_gather(shards[1], "fsdp", axis=0, tiled=True),
            lax.all_gather(shards[2], "fsdp", axis=0, tiled=True),
            lax.all_gather(shards[3], "fsdp", axis=0, tiled=True),
            lax.all_gather(shards[4], "fsdp", axis=0, tiled=True),
            lax.all_gather(shards[5], "fsdp", axis=0, tiled=True),
            lax.all_gather(shards[6], "fsdp", axis=0, tiled=True),
            lax.all_gather(shards[7], "fsdp", axis=0, tiled=True),
            lax.all_gather(shards[8], "fsdp", axis=0, tiled=True),
            lax.all_gather(shards[9], "fsdp", axis=0, tiled=True),
            lax.all_gather(shards[10], "fsdp", axis=0, tiled=True),
            lax.all_gather(shards[11], "fsdp", axis=0, tiled=True),
            lax.all_gather(shards[12], "fsdp", axis=0, tiled=True),
            lax.all_gather(shards[13], "fsdp", axis=0, tiled=True),
            lax.all_gather(shards[14], "fsdp", axis=0, tiled=True),
            lax.all_gather(shards[15], "fsdp", axis=0, tiled=True),
            lax.all_gather(shards[16], "fsdp", axis=0, tiled=True),
        )

        def forward_one(item_pack):
            return image_forward(forward_params, item_pack[0], item_pack[1])

        pooled, saved = lax.map(forward_one, (tokens[micro_step], lengths[micro_step]))
        backward_params = (
            lax.all_gather(shards[0], "fsdp", axis=0, tiled=True),
            lax.all_gather(shards[1], "fsdp", axis=0, tiled=True),
            lax.all_gather(shards[2], "fsdp", axis=0, tiled=True),
            lax.all_gather(shards[3], "fsdp", axis=0, tiled=True),
            lax.all_gather(shards[4], "fsdp", axis=0, tiled=True),
            lax.all_gather(shards[5], "fsdp", axis=0, tiled=True),
            lax.all_gather(shards[6], "fsdp", axis=0, tiled=True),
            lax.all_gather(shards[7], "fsdp", axis=0, tiled=True),
            lax.all_gather(shards[8], "fsdp", axis=0, tiled=True),
            lax.all_gather(shards[9], "fsdp", axis=0, tiled=True),
            lax.all_gather(shards[10], "fsdp", axis=0, tiled=True),
            lax.all_gather(shards[11], "fsdp", axis=0, tiled=True),
            lax.all_gather(shards[12], "fsdp", axis=0, tiled=True),
            lax.all_gather(shards[13], "fsdp", axis=0, tiled=True),
            lax.all_gather(shards[14], "fsdp", axis=0, tiled=True),
            lax.all_gather(shards[15], "fsdp", axis=0, tiled=True),
            lax.all_gather(shards[16], "fsdp", axis=0, tiled=True),
        )
        grad_zero = tuple((jnp.zeros(item.shape, jnp.float32) for item in backward_params))

        def backward_one(grad_carry, item_pack):
            d_image, grad_parts = image_backward(
                backward_params, item_pack[0], item_pack[1], item_pack[2], item_pack[3]
            )
            return (tuple((left + right for left, right in zip(grad_carry, grad_parts))), d_image)

        micro_grads, d_images = lax.scan(
            backward_one,
            grad_zero,
            (tokens[micro_step], lengths[micro_step], cotangent[micro_step], saved),
        )
        if grad_total is None:
            grad_total = micro_grads
        else:
            grad_total = tuple((left + right for left, right in zip(grad_total, micro_grads)))
        pooled_parts.append(pooled)
        grad_image_parts.append(d_images)
    flat_terms = jnp.concatenate([item.reshape(devices, -1) for item in grad_total], axis=1)
    summed = lax.psum_scatter(flat_terms.reshape(-1), "fsdp", scatter_dimension=0, tiled=True)
    grad_total = unflatten_all(summed, grad_total, devices)
    return (jnp.stack(pooled_parts), jnp.stack(grad_image_parts)) + tuple(grad_total)


def solution(mesh):
    placed = (
        P(None, "fsdp", None, None),
        P(None, "fsdp"),
        P(None, "fsdp", None, None),
        P("fsdp"),
        P("fsdp"),
        P("fsdp", None),
        P("fsdp"),
        P("fsdp", None),
        P("fsdp"),
        P("fsdp"),
        P("fsdp"),
        P("fsdp", None),
        P("fsdp"),
        P("fsdp", None),
        P("fsdp"),
        P("fsdp"),
        P("fsdp"),
        P("fsdp", None),
        P("fsdp"),
        P("fsdp", None),
    )
    return jax.shard_map(
        body,
        mesh=mesh,
        in_specs=placed,
        out_specs=(
            P(None, "fsdp", None, None),
            P(None, "fsdp", None, None),
            P("fsdp"),
            P("fsdp"),
            P("fsdp", None),
            P("fsdp"),
            P("fsdp", None),
            P("fsdp"),
            P("fsdp"),
            P("fsdp"),
            P("fsdp", None),
            P("fsdp"),
            P("fsdp", None),
            P("fsdp"),
            P("fsdp"),
            P("fsdp"),
            P("fsdp", None),
            P("fsdp"),
            P("fsdp", None),
        ),
        check_vma=False,
    )
```

profile of v0, /device:TPU:0, one launch (start us, length us, event | category | flops | bytes accessed | tf_op | source)
XLA Modules:
  0.0 1819.9 jit_solution(6046457286659416338)
XLA Ops:
  26.6 42.9 %all-reduce.11 = (bf16[2048]{0:T(1024)(128)(2,1)S(1)}, bf16[1024]{0:T(1024)(128)(2,1)S(1)}, bf16[1024]{0:T(1024)(128)(2,1)S(1)}, bf16[1024]{0:T(1024)(128)(2,1)S...) all-reduce(bf16[2048]{0:T(1024)(128)(2,1)S(1)} %dynamic-update-slic, ...), channel_id=1, replica_groups=mesh['fsdp'=32] {'fsdp'}, use_global_device_ids=true, to_apply=%add.2 | all-reduce | flops 11264 | bytes 45056
  76.5 40.1 %all-gather = bf16[32,1,128]{2,1,0:T(2,128)(2,1)S(1)} all-gather(bf16[1,1,128]{2,1,0:T(2,128)(2,1)S(1)} %bitcast.258), channel_id=1, replica_groups=mesh['fsdp'=32] {'fsdp'}, dimensions={0}, use_global_device_ids=true | all-gather | bytes 8448 | tf_op jit(solution)/shard_map/all_gather | solution.py:328
  117.3 37.0 %all-gather.1 = bf16[32,32,8]{1,2,0:T(8,128)(2,1)S(1)} all-gather(bf16[1,32,8]{1,2,0:T(8,128)(2,1)S(1)} %bitcast.257), channel_id=1, replica_groups=mesh['fsdp'=32] {'fsdp'}, dimensions={0}, use_global_device_ids=true | all-gather | bytes 16896 | tf_op jit(solution)/shard_map/all_gather | solution.py:335
  187.0 14.6 fusion
  288.6 53.1 %multiply_convert_fusion.3 = (bf16[576,4096]{1,0:T(8,128)(2,1)}, f32[576,4096]{1,0:T(8,128)}, bf16[576,4096]{1,0:T(8,128)(2,1)}, f32[576,4096]{1,0:T(8,128)}, f32[576,4096]{1,0:T(8,128)}) fusion(f32[4096]{0:T(1024)S(1)} %bitcast.254, f32[576,4096]{1,0:T(8,128)S(1)} %fusion.126, bf16[1024,4096]{1,0:T(8,128)(2,1)S(1)} %copy-done.133, ...), kind=kOutput, calls=%fused_computation.35 | convolution fusion | flops 5146214400 | bytes 57963008 | tf_op jit(solution)/shard_map/while/body/eval_jaxpr/dot_general | solution.py:35
  410.6 17.2 convert_reduce_fusion.1
  427.8 13.0 fusion.122
  453.1 17.3 convert_reduce_fusion
  470.5 14.1 multiply_reduce_fusion.4
  505.8 16.8 multiply_reduce_fusion
  522.6 20.2 %multiply_convert_fusion = bf16[16,576,576]{1,2,0:T(8,128)(2,1)} fusion(f32[16,576,576]{1,2,0:T(8,128)} %get-tuple-element.659, f32[16,576,576]{1,2,0:T(8,128)} %get-tuple-element.595, f32[16,576]{1,0:T(8,128)S(1)} %get-tuple-element.658, f32[16,576]{1,0:T(8,128)S(1)} %copy-done.56, pred[576]{0:T(1024)(128)(4,1)S(1)} %copy-done.101), kind=kLoop, calls=%fused_computation | loop fusion | flops 31850496 | bytes 53158464 | tf_op jit(solution)/shard_map/while/body/eval_jaxpr/convert_element_type | solution.py:220
  577.6 16.2 multiply_reduce_fusion.1
  593.8 20.7 %multiply_convert_fusion.1 = bf16[16,576,576]{1,2,0:T(8,128)(2,1)} fusion(f32[16,576,576]{1,2,0:T(8,128)} %get-tuple-element.657, f32[16,576,576]{1,2,0:T(8,128)} %get-tuple-element.597, f32[16,576]{1,0:T(8,128)S(1)} %get-tuple-element.656, f32[16,576]{1,0:T(8,128)S(1)} %copy-done.54, pred[576]{0:T(1024)(128)(4,1)S(1)} %copy-done.99), kind=kLoop, calls=%fused_computation.2 | loop fusion | flops 31850496 | bytes 53158464 | tf_op jit(solution)/shard_map/while/body/eval_jaxpr/convert_element_type | solution.py:220
  656.0 15.2 convolution_add_fusion
  671.2 12.4 reshape.578
  683.6 15.0 convolution_add_fusion.1
  698.6 12.4 reshape.579
  748.3 15.8 convolution_add_fusion.2
  777.0 37.1 %dynamic-update-slice.12 = f32[32,426720]{1,0:T(8,128)} dynamic-update-slice(f32[32,426720]{1,0:T(8,128)} %dynamic-update-slice.11, f32[32,98304]{1,0:T(8,128)} %reshape.576, s32[]{} %constant.650, s32[]{} %constant.652) | dynamic-update-slice | bytes 25165828
  824.4 48.2 %dynamic-update-slice.18 = f32[32,426720]{1,0:T(8,128)} dynamic-update-slice(f32[32,426720]{1,0:T(8,128)} %dynamic-update-slice.17, f32[32,131072]{1,0:T(8,128)} %reshape.578, s32[]{} %constant.650, s32[]{} %constant.658) | dynamic-update-slice | bytes 33554436
  874.1 48.2 %dynamic-update-slice.20 = f32[32,426720]{1,0:T(8,128)} dynamic-update-slice(f32[32,426720]{1,0:T(8,128)} %dynamic-update-slice.19, f32[32,131072]{1,0:T(8,128)} %reshape.579, s32[]{} %constant.650, s32[]{} %constant.660) | dynamic-update-slice | bytes 33554436
  926.6 14.3 dynamic-update-slice.24
  944.1 77.3 %reshape.582 = f32[13655040]{0:T(1024)} reshape(f32[32,426720]{1,0:T(8,128)} %dynamic-update-slice.26) | data formatting | bytes 109240320 | tf_op jit(solution)/shard_map/reshape | solution.py:381
  1031.8 767.8 %all-reduce.14.cloned.1.call-done = f32[13655040]{0:T(1024)} async-done(((f32[13655040]{0:T(1024)}), f32[13655040]{0:T(1024)}) %all-reduce.14.cloned.1.call-update) | async-done | bytes 54620176
  (505 shorter events, 415.9 us)
Async XLA Ops:
  7.2 67.9 %copy-start.4 = (bf16[2,1,576,1024]{3,2,1,0:T(8,128)(2,1)S(1)}, bf16[2,1,576,1024]{3,2,1,0:T(8,128)(2,1)}, u32[]{:S(2)}) copy-start(bf16[2,1,576,1024]{3,2,1,0:T(8,128)(2,1)} %param.20) | copy-start | bytes 7077892
  7.2 147.9 %all-gather.8.cloned.1.call-start = ((), (), s32[]{:S(2)}) async-start(), calls=%async_computation | async-start | bytes 6488064 | tf_op jit(solution)/shard_map/all_gather | solution.py:321
  7.9 222.9 %all-gather.10.cloned.1.call-start = ((), (), s32[]{:S(2)}) async-start(), calls=%async_computation.1 | async-start | bytes 2162688 | tf_op jit(solution)/shard_map/all_gather | solution.py:323
  8.7 267.7 %all-gather.12.cloned.1.call-start = ((), (), s32[]{:S(2)}) async-start(), calls=%async_computation.2 | async-start | bytes 8650752 | tf_op jit(solution)/shard_map/all_gather | solution.py:327
  9.4 332.2 %all-gather.14.cloned.1.call-start = ((), (), s32[]{:S(2)}) async-start(), calls=%async_computation.3 | async-start | bytes 8650752 | tf_op jit(solution)/shard_map/all_gather | solution.py:329
  10.0 351.3 %all-gather.16.cloned.1.call-start = ((), (), s32[]{:S(2)}) async-start(), calls=%async_computation.4 | async-start | bytes 2162688 | tf_op jit(solution)/shard_map/all_gather | solution.py:333
  10.6 1789.0 %all-reduce.14.cloned.1.call-start = ((), (), s32[]{:S(2)}) async-start(), calls=%async_computation.5 | async-start | bytes 109240320
  69.4 96.3 %copy-start.76 = (f32[1024]{0:T(1024)}, f32[1024]{0:T(1024)S(1)}, u32[]{:S(2)}) copy-start(f32[1024]{0:T(1024)S(1)} %convert_element_type.370) | copy-start | bytes 12292
  70.0 85.1 %copy-start.124 = (f32[1024]{0:T(1024)}, f32[1024]{0:T(1024)S(1)}, u32[]{:S(2)}) copy-start(f32[1024]{0:T(1024)S(1)} %convert_element_type.371) | copy-start | bytes 12292
  70.0 357.7 %copy-start.57 = (f32[1024]{0:T(1024)}, f32[1024]{0:T(1024)S(1)}, u32[]{:S(2)}) copy-start(f32[1024]{0:T(1024)S(1)} %convert_element_type.382) | copy-start | bytes 12292
  73.0 44.3 %copy-start.131 = (bf16[32,8]{0,1:T(8,128)(2,1)S(1)}, bf16[32,8]{0,1:T(8,128)(2,1)}, u32[]{:S(2)}) copy-start(bf16[32,8]{0,1:T(8,128)(2,1)} %param.39) | copy-start | bytes 1540
  75.1 80.0 %copy-start.66 = (f32[576]{0:T(1024)}, f32[576]{0:T(1024)S(1)}, u32[]{:S(2)}) copy-start(f32[576]{0:T(1024)S(1)} %get-tuple-element.677) | copy-start | bytes 6916
  75.1 90.6 %copy-start.68 = (f32[576]{0:T(1024)}, f32[576]{0:T(1024)S(1)}, u32[]{:S(2)}) copy-start(f32[576]{0:T(1024)S(1)} %get-tuple-element.678) | copy-start | bytes 6916
  76.5 78.6 %copy-start.78 = (f32[576]{0:T(1024)}, f32[576]{0:T(1024)S(1)}, u32[]{:S(2)}) copy-start(f32[576]{0:T(1024)S(1)} %fusion.96) | copy-start | bytes 6916
  288.6 53.1 %copy-start.129 = (f32[1024]{0:T(1024)S(1)}, f32[1024]{0:T(1024)}, u32[]{:S(2)}) copy-start(f32[1024]{0:T(1024)} %convert_element_type.386) | copy-start | bytes 12292
  351.7 44.3 %copy-start.6 = (f32[576,1024]{1,0:T(8,128)}, f32[576,1024]{1,0:T(8,128)S(1)}, u32[]{:S(2)}) copy-start(f32[576,1024]{1,0:T(8,128)S(1)} %get-tuple-element.650) | copy-start | bytes 7077892
  359.4 36.5 %copy-start.93 = (f32[576]{0:T(1024)}, f32[576]{0:T(1024)S(1)}, u32[]{:S(2)}) copy-start(f32[576]{0:T(1024)S(1)} %broadcast_multiply_fusion) | copy-start | bytes 6916
  361.2 34.7 %copy-start.111 = (f32[576]{0:T(1024)}, f32[576]{0:T(1024)S(1)}, u32[]{:S(2)}) copy-start(f32[576]{0:T(1024)S(1)} %fusion.98) | copy-start | bytes 6916
  381.3 59.5 %copy-start.61 = (f32[576,8]{0,1:T(8,128)}, f32[576,8]{0,1:T(8,128)S(1)}, u32[]{:S(2)}) copy-start(f32[576,8]{0,1:T(8,128)S(1)} %fusion.65) | copy-start | bytes 55300
  400.3 160.1 %copy-start.14 = (f32[576,1024]{1,0:T(8,128)}, f32[576,1024]{1,0:T(8,128)S(1)}, u32[]{:S(2)}) copy-start(f32[576,1024]{1,0:T(8,128)S(1)} %add_add_fusion.9) | copy-start | bytes 7077892
  443.1 47.1 %copy-start.11 = (f32[576,1024]{1,0:T(8,128)}, f32[576,1024]{1,0:T(8,128)S(1)}, u32[]{:S(2)}) copy-start(f32[576,1024]{1,0:T(8,128)S(1)} %add_add_fusion.7) | copy-start | bytes 7077892
  777.0 37.1 %copy-start.95 = (f32[16,64]{1,0:T(8,128)S(1)}, f32[16,64]{1,0:T(8,128)}, u32[]{:S(2)}) copy-start(f32[16,64]{1,0:T(8,128)} %get-tuple-element.667) | copy-start | bytes 12292
  777.0 37.1 %copy-start.96 = (f32[16,64]{1,0:T(8,128)S(1)}, f32[16,64]{1,0:T(8,128)}, u32[]{:S(2)}) copy-start(f32[16,64]{1,0:T(8,128)} %get-tuple-element.665) | copy-start | bytes 12292
  777.0 37.1 %copy-start.97 = (f32[16,64]{1,0:T(8,128)S(1)}, f32[16,64]{1,0:T(8,128)}, u32[]{:S(2)}) copy-start(f32[16,64]{1,0:T(8,128)} %get-tuple-element.661) | copy-start | bytes 12292
  (130 other events, 922.0 us)
Sparse Core Ops, SparseCore 0:
  10.9 73.0 all-gather.7
  86.8 54.9 all-gather.9
  144.7 76.3 all-gather.11
  223.8 76.0 all-gather.13
  302.6 55.0 all-gather.15
  1021.6 777.9 all-reduce.13
where the time goes:
time: 1830 us; the launch traced here: 1820 us
  waiting for transfers between devices  771 us (42%)
  matrix products  433 us (24%)
  local copies, waits for them, and re-layouts  363 us (20%)
  blocking collectives  120 us (7%)
  other arithmetic  116 us (6%)
    unnamed x7, waiting for transfers between devices  771 us
    unnamed x334, local copies, waits for them, and re-layouts  207 us
    dot_general x12, matrix products, product(): return jnp.dot(left, right, preferred_element_type=jnp.float32)  112 us
    dot_general x12, matrix products, product_rows(): lax.dot_general(left, right, (((0,), (0,)), ((), ())), preferred_element_...  103 us
    dot_general x12, matrix products, product_back(): lax.dot_general(left, right, (((1,), (1,)), ((), ())), preferred_element_...  83.8 us
    reshape x1, local copies, waits for them, and re-layouts, body(): flat_terms.reshape(-1)  77.3 us
    reshape x6, local copies, waits for them, and re-layouts, body(): item.reshape(devices, -1)  45.1 us
    unnamed x1, blocking collectives  42.9 us
  transfers between devices with their start and end apart: 6, of which 1 were waited for; matrix products, arithmetic and copies ran while one was open for 12% of the time, Pallas kernels for 0%

commit v1 on v0

--- a/solution.py
+++ b/solution.py
@@ -8,6 +8,18 @@
 HD = 64
 EPSILON = 1e-06
 SCALE = 0.125
+
+
+def collect(x, axis, dim):
+    ways, here, step = (lax.axis_size(axis), lax.axis_index(axis), x.shape[dim])
+    line, have = (x, 1)
+    while have < ways:
+        line = jnp.concatenate(
+            [line, lax.ppermute(line, axis, [(d, (d - have) % ways) for d in range(ways)])],
+            axis=dim,
+        )
+        have = 2 * have
+    return jnp.roll(line, here * step, axis=dim)
 
 
 def layer_norm(values, gain, shift):
@@ -325,7 +337,7 @@
             lax.all_gather(shards[6], "fsdp", axis=0, tiled=True),
             lax.all_gather(shards[7], "fsdp", axis=0, tiled=True),
             lax.all_gather(shards[8], "fsdp", axis=0, tiled=True),
-            lax.all_gather(shards[9], "fsdp", axis=0, tiled=True),
+            collect(shards[9], "fsdp", 0),
             lax.all_gather(shards[10], "fsdp", axis=0, tiled=True),
             lax.all_gather(shards[11], "fsdp", axis=0, tiled=True),
             lax.all_gather(shards[12], "fsdp", axis=0, tiled=True),

time: 1830 us -> 1830 us (level)
  blocking collectives: 120 us -> 82.2 us
    all_gather x1 -> x0, blocking collectives: 40.1 us -> none  [body(): lax.all_gather(shards[9], 'fsdp', axis=0, tiled=True)]
    unnamed x334 -> x344, local copies, waits for them, and re-layouts: 207 us -> 210 us
  transfers between devices with their start and end apart: 6 -> 11, of which waited for: 1 -> 4; matrix products, arithmetic and copies ran while one was open for 12% -> 12% of each run, Pallas kernels for 0% -> 0%
where the time goes in v1:
time: 1830 us; the launch traced here: 1820 us
  waiting for transfers between devices  787 us (43%)
  matrix products  433 us (24%)
  local copies, waits for them, and re-layouts  366 us (20%)
  other arithmetic  115 us (6%)
  blocking collectives  82.2 us (4%)
    unnamed x7, waiting for transfers between devices  770 us
    unnamed x344, local copies, waits for them, and re-layouts  210 us
    dot_general x12, matrix products, product(): return jnp.dot(left, right, preferred_element_type=jnp.float32)  111 us
    dot_general x12, matrix products, product_rows(): lax.dot_general(left, right, (((0,), (0,)), ((), ())), preferred_element_...  103 us
    dot_general x12, matrix products, product_back(): lax.dot_general(left, right, (((1,), (1,)), ((), ())), preferred_element_...  83.8 us
    reshape x1, local copies, waits for them, and re-layouts, body(): flat_terms.reshape(-1)  77.3 us
    reshape x6, local copies, waits for them, and re-layouts, body(): item.reshape(devices, -1)  45.2 us
    all_gather x1, blocking collectives, body(): lax.all_gather(shards[16], 'fsdp', axis=0, tiled=True)  44.6 us
  transfers between devices with their start and end apart: 11, of which 4 were waited for; matrix products, arithmetic and copies ran while one was open for 12% of the time, Pallas kernels for 0%

profile of v1, /device:TPU:0, one launch (start us, length us, event | category | flops | bytes accessed | tf_op | source)
XLA Modules:
  0.0 1815.5 jit_solution(15589106332429572018)
XLA Ops:
  26.9 37.6 %all-reduce.11 = (bf16[2048]{0:T(1024)(128)(2,1)S(1)}, bf16[1024]{0:T(1024)(128)(2,1)S(1)}, bf16[1024]{0:T(1024)(128)(2,1)S(1)}, bf16[1024]{0:T(1024)(128)(2,1)S...) all-reduce(bf16[2048]{0:T(1024)(128)(2,1)S(1)} %dynamic-update-slic, ...), channel_id=1, replica_groups=mesh['fsdp'=32] {'fsdp'}, use_global_device_ids=true, to_apply=%add.2 | all-reduce | flops 11264 | bytes 45056
  84.8 44.6 %all-gather = bf16[32,32,8]{1,2,0:T(8,128)(2,1)S(1)} all-gather(bf16[1,32,8]{1,2,0:T(8,128)(2,1)S(1)} %bitcast.252), channel_id=1, replica_groups=mesh['fsdp'=32] {'fsdp'}, dimensions={0}, use_global_device_ids=true | all-gather | bytes 16896 | tf_op jit(solution)/shard_map/all_gather | solution.py:347
  166.1 14.6 fusion
  268.1 53.1 %multiply_convert_fusion.3 = (bf16[576,4096]{1,0:T(8,128)(2,1)}, f32[576,4096]{1,0:T(8,128)}, bf16[576,4096]{1,0:T(8,128)(2,1)}, f32[576,4096]{1,0:T(8,128)}, f32[576,4096]{1,0:T(8,128)}) fusion(f32[4096]{0:T(1024)S(1)} %copy-done.107, f32[576,4096]{1,0:T(8,128)S(1)} %fusion.128, bf16[1024,4096]{1,0:T(8,128)(2,1)S(1)} %copy-done.134, ...), kind=kOutput, calls=%fused_computation.35 | convolution fusion | flops 5146214400 | bytes 57963008 | tf_op jit(solution)/shard_map/while/body/eval_jaxpr/dot_general | solution.py:47
  340.5 17.0 all-gather.15.cloned.1.call-done
  406.8 17.2 convert_reduce_fusion.1
  424.0 13.0 fusion.124
  449.3 17.3 convert_reduce_fusion
  466.7 14.1 multiply_reduce_fusion.4
  501.9 16.8 multiply_reduce_fusion
  518.7 20.3 %multiply_convert_fusion = bf16[16,576,576]{1,2,0:T(8,128)(2,1)} fusion(f32[16,576,576]{1,2,0:T(8,128)} %get-tuple-element.662, f32[16,576,576]{1,2,0:T(8,128)} %get-tuple-element.598, f32[16,576]{1,0:T(8,128)S(1)} %get-tuple-element.661, f32[16,576]{1,0:T(8,128)S(1)} %copy-done.56, pred[576]{0:T(1024)(128)(4,1)S(1)} %copy-done.102), kind=kLoop, calls=%fused_computation | loop fusion | flops 31850496 | bytes 53158464 | tf_op jit(solution)/shard_map/while/body/eval_jaxpr/convert_element_type | solution.py:232
  573.7 16.2 multiply_reduce_fusion.1
  589.9 20.7 %multiply_convert_fusion.1 = bf16[16,576,576]{1,2,0:T(8,128)(2,1)} fusion(f32[16,576,576]{1,2,0:T(8,128)} %get-tuple-element.660, f32[16,576,576]{1,2,0:T(8,128)} %get-tuple-element.600, f32[16,576]{1,0:T(8,128)S(1)} %get-tuple-element.659, f32[16,576]{1,0:T(8,128)S(1)} %copy-done.54, pred[576]{0:T(1024)(128)(4,1)S(1)} %copy-done.100), kind=kLoop, calls=%fused_computation.2 | loop fusion | flops 31850496 | bytes 53158464 | tf_op jit(solution)/shard_map/while/body/eval_jaxpr/convert_element_type | solution.py:232
  652.2 15.2 convolution_add_fusion
  667.5 12.4 reshape.578
  679.9 15.0 convolution_add_fusion.1
  695.0 12.4 reshape.579
  744.7 15.9 convolution_add_fusion.2
  773.4 37.1 %dynamic-update-slice.12 = f32[32,426720]{1,0:T(8,128)} dynamic-update-slice(f32[32,426720]{1,0:T(8,128)} %dynamic-update-slice.11, f32[32,98304]{1,0:T(8,128)} %reshape.576, s32[]{} %constant.673, s32[]{} %constant.675) | dynamic-update-slice | bytes 25165828
  820.8 48.1 %dynamic-update-slice.18 = f32[32,426720]{1,0:T(8,128)} dynamic-update-slice(f32[32,426720]{1,0:T(8,128)} %dynamic-update-slice.17, f32[32,131072]{1,0:T(8,128)} %reshape.578, s32[]{} %constant.673, s32[]{} %constant.681) | dynamic-update-slice | bytes 33554436
  870.5 48.2 %dynamic-update-slice.20 = f32[32,426720]{1,0:T(8,128)} dynamic-update-slice(f32[32,426720]{1,0:T(8,128)} %dynamic-update-slice.19, f32[32,131072]{1,0:T(8,128)} %reshape.579, s32[]{} %constant.673, s32[]{} %constant.683) | dynamic-update-slice | bytes 33554436
  923.0 14.3 dynamic-update-slice.24
  940.6 77.3 %reshape.582 = f32[13655040]{0:T(1024)} reshape(f32[32,426720]{1,0:T(8,128)} %dynamic-update-slice.26) | data formatting | bytes 109240320 | tf_op jit(solution)/shard_map/reshape | solution.py:393
  1028.1 767.0 %all-reduce.14.cloned.1.call-done = f32[13655040]{0:T(1024)} async-done(((f32[13655040]{0:T(1024)}), f32[13655040]{0:T(1024)}) %all-reduce.14.cloned.1.call-update) | async-done | bytes 54620176
  (531 shorter events, 432.9 us)
Async XLA Ops:
  7.2 60.0 %copy-start.4 = (bf16[2,1,576,1024]{3,2,1,0:T(8,128)(2,1)S(1)}, bf16[2,1,576,1024]{3,2,1,0:T(8,128)(2,1)}, u32[]{:S(2)}) copy-start(bf16[2,1,576,1024]{3,2,1,0:T(8,128)(2,1)} %param.22) | copy-start | bytes 7077892
  7.2 126.7 %all-gather.7.cloned.1.call-start = ((), (), s32[]{:S(2)}) async-start(), calls=%async_computation | async-start | bytes 6488064 | tf_op jit(solution)/shard_map/all_gather | solution.py:333
  7.9 202.6 %all-gather.9.cloned.1.call-start = ((), (), s32[]{:S(2)}) async-start(), calls=%async_computation.1 | async-start | bytes 2162688 | tf_op jit(solution)/shard_map/all_gather | solution.py:335
  8.7 247.2 %all-gather.11.cloned.1.call-start = ((), (), s32[]{:S(2)}) async-start(), calls=%async_computation.2 | async-start | bytes 8650752 | tf_op jit(solution)/shard_map/all_gather | solution.py:339
  9.4 311.7 %all-gather.13.cloned.1.call-start = ((), (), s32[]{:S(2)}) async-start(), calls=%async_computation.3 | async-start | bytes 8650752 | tf_op jit(solution)/shard_map/all_gather | solution.py:341
  10.0 347.4 %all-gather.15.cloned.1.call-start = ((), (), s32[]{:S(2)}) async-start(), calls=%async_computation.4 | async-start | bytes 2162688 | tf_op jit(solution)/shard_map/all_gather | solution.py:345
  10.0 60.0 %collective-permute-start = (bf16[128]{0:T(256)(128)(2,1)}, bf16[128]{0:T(256)(128)(2,1)S(1)}, u32[]{:S(2)}, u32[]{:S(2)}) collective-permute-start(bf16[128]{0:T(256)(128)(2,1)} %param.34), channel_id=1, source_target_pairs={{0,31},{1,0},{2,1},{3,2},{4,3},{5,4},{6,5},{7,6},{8,7},{9,8},{10,9... | collective-permute-start | bytes 776 | tf_op jit(solution)/shard_map/ppermute | solution.py:18
  16.5 1778.7 %all-reduce.14.cloned.1.call-start = ((), (), s32[]{:S(2)}) async-start(), calls=%async_computation.5 | async-start | bytes 109240320
  67.2 66.7 %copy-start.66 = (f32[576]{0:T(1024)}, f32[576]{0:T(1024)S(1)}, u32[]{:S(2)}) copy-start(f32[576]{0:T(1024)S(1)} %get-tuple-element.680) | copy-start | bytes 6916
  67.2 77.5 %copy-start.68 = (f32[576]{0:T(1024)}, f32[576]{0:T(1024)S(1)}, u32[]{:S(2)}) copy-start(f32[576]{0:T(1024)S(1)} %get-tuple-element.681) | copy-start | bytes 6916
  68.0 63.8 %copy-start.82 = (f32[576]{0:T(1024)}, f32[576]{0:T(1024)S(1)}, u32[]{:S(2)}) copy-start(f32[576]{0:T(1024)S(1)} %get-tuple-element.475) | copy-start | bytes 6916
  68.0 63.8 %copy-start.84 = (f32[576]{0:T(1024)}, f32[576]{0:T(1024)S(1)}, u32[]{:S(2)}) copy-start(f32[576]{0:T(1024)S(1)} %get-tuple-element.474) | copy-start | bytes 6916
  68.0 76.6 %copy-start.78 = (f32[576]{0:T(1024)}, f32[576]{0:T(1024)S(1)}, u32[]{:S(2)}) copy-start(f32[576]{0:T(1024)S(1)} %fusion.95) | copy-start | bytes 6916
  68.0 65.8 %copy-start.76 = (f32[576]{0:T(1024)}, f32[576]{0:T(1024)S(1)}, u32[]{:S(2)}) copy-start(f32[576]{0:T(1024)S(1)} %fusion.98) | copy-start | bytes 6916
  70.1 5.1 collective-permute-start.1
  75.1 3.9 collective-permute-start.2
  79.1 5.0 collective-permute-start.3
  84.1 49.0 %collective-permute-start.4 = (bf16[2048]{0:T(1024)(128)(2,1)S(1)}, bf16[2048]{0:T(1024)(128)(2,1)S(1)}, u32[]{:S(2)}, u32[]{:S(2)}) collective-permute-start(bf16[2048]{0:T(1024)(128)(2,1)S(1)} %get-tuple-element.593), channel_id=1, source_target_pairs={{0,16},{1,17},{2,18},{3,19},{4,20},{5,21},{6,22},{7,23},{8,24},{9,... | collective-permute-start | bytes 12296 | tf_op jit(solution)/shard_map/ppermute | solution.py:18
  130.0 293.9 %copy-start.57 = (f32[1024]{0:T(1024)}, f32[1024]{0:T(1024)S(1)}, u32[]{:S(2)}) copy-start(f32[1024]{0:T(1024)S(1)} %convert_element_type.382) | copy-start | bytes 12292
  268.1 53.1 %copy-start.131 = (f32[1024]{0:T(1024)S(1)}, f32[1024]{0:T(1024)}, u32[]{:S(2)}) copy-start(f32[1024]{0:T(1024)} %convert_element_type.386) | copy-start | bytes 12292
  330.9 61.2 %copy-start.6 = (f32[576,1024]{1,0:T(8,128)}, f32[576,1024]{1,0:T(8,128)S(1)}, u32[]{:S(2)}) copy-start(f32[576,1024]{1,0:T(8,128)S(1)} %get-tuple-element.653) | copy-start | bytes 7077892
  338.6 53.4 %copy-start.94 = (f32[576]{0:T(1024)}, f32[576]{0:T(1024)S(1)}, u32[]{:S(2)}) copy-start(f32[576]{0:T(1024)S(1)} %broadcast_multiply_fusion) | copy-start | bytes 6916
  377.4 59.6 %copy-start.61 = (f32[576,8]{0,1:T(8,128)}, f32[576,8]{0,1:T(8,128)S(1)}, u32[]{:S(2)}) copy-start(f32[576,8]{0,1:T(8,128)S(1)} %fusion.65) | copy-start | bytes 55300
  396.4 160.1 %copy-start.14 = (f32[576,1024]{1,0:T(8,128)}, f32[576,1024]{1,0:T(8,128)S(1)}, u32[]{:S(2)}) copy-start(f32[576,1024]{1,0:T(8,128)S(1)} %add_add_fusion.9) | copy-start | bytes 7077892
  (136 other events, 1210.9 us)
Sparse Core Ops, SparseCore 0:
  10.9 73.0 all-gather.6
  86.9 54.8 all-gather.8
  144.6 76.2 all-gather.10
  223.6 76.0 all-gather.12
  302.4 54.9 all-gather.14
  1018.0 777.1 all-reduce.13
